TPU v7x, 256 devices: a whole 4x4x8 slice. The times are simulated.
256 devices in a mesh: grp: 8 (over x_hi, y), blk: 32 (over x_lo, z, core).
Axes of the slice: x: 4 (x_hi: 2, x_lo: 2; x = x_hi * 2 + x_lo), y: 4, z: 8, core: 2. Of those that a mesh axis runs over, the one named last changes fastest.
Arguments:
- queries: bfloat16 [32768, 4096], P(('grp', 'blk')), parts along dimension 0, may hold values from -256 to 256
- new_keys: bfloat16 [32768, 512], P(('grp', 'blk')), parts along dimension 0, may hold values from -6 to 6
- new_values: bfloat16 [32768, 512], P(('grp', 'blk')), parts along dimension 0, may hold values from -6 to 6
- prefix_keys: bfloat16 [32768, 512], P(('grp', 'blk')), parts along dimension 0, may hold values from -6 to 6
- prefix_values: bfloat16 [32768, 512], P(('grp', 'blk')), parts along dimension 0, may hold values from -6 to 6
- block_table: int32 [256, 16], P(('grp', 'blk')), parts along dimension 0, may hold values from 0 to 31, as said below
- prefix_blocks: int32 [256], P(('grp', 'blk')), parts along dimension 0, may hold values from 1 to 16, 320 in all
Outputs:
- attended: bfloat16 [32768, 4096], P(('grp', 'blk')), parts along dimension 0
There are 8 independent parts, one for each index of `grp`. A program takes and returns all parts, laid end to end along the dimension named above; each array names one. Nothing has to cross between parts.
Inputs may be any that keep to these rules, and one draw needn't show every extreme that they name: `block_table`: each row names 16 different prefix blocks; only the first prefix_blocks entries of a row are read. `prefix_blocks`: within each group (each index of grp) the lengths sum to 320.
All inputs are finite; a program needn't handle non-finite values.
Results may differ from a plain program's by a relative error of at most 0.008.
Values may be sent and summed in bfloat16 or wider, within the bound.
No kernel may reach another device: no remote copies, remote signals or barrier semaphores. Data moves between devices by JAX's collectives and lax.ppermute only.
A program may use at most 64 MiB of HBM per device.

v0:
```python
import jax
import jax.numpy as jnp
from jax import lax
from jax.sharding import PartitionSpec as P

KVH = 4
DH = 128
BS = 128
G = 8


def head_major(block, heads):
    rows = block.shape[0]
    return block.reshape(rows, heads, DH).transpose(1, 0, 2)


def absorb(carry, key_block, value_block, usable, query_heads):
    top, total, summed = carry
    scores = jnp.einsum(
        "krd,kld->krl", query_heads, key_block, preferred_element_type=jnp.float32
    ) * DH ** (-0.5)
    scores = jnp.where(usable, scores, -jnp.inf)
    new_top = jnp.maximum(top, jnp.max(scores, axis=-1))
    factor = jnp.exp(top - new_top)
    weights = jnp.exp(scores - new_top[..., None])
    total = factor * total + jnp.sum(weights, axis=-1)
    summed = factor[..., None] * summed + jnp.einsum(
        "krl,kld->krd",
        weights.astype(jnp.bfloat16),
        value_block,
        preferred_element_type=jnp.float32,
    )
    return (new_top, total, summed)


def body(queries, new_keys, new_values, prefix_keys, prefix_values, block_table, prefix_blocks):
    tokens = queries.shape[0]
    query_heads = (
        queries.reshape(tokens, KVH, G, DH).transpose(1, 2, 0, 3).reshape(KVH, G * tokens, DH)
    )
    own_keys = head_major(new_keys, KVH)
    own_values = head_major(new_values, KVH)
    scores = jnp.einsum(
        "krd,kld->krl", query_heads, own_keys, preferred_element_type=jnp.float32
    ) * DH ** (-0.5)
    row_token = jnp.arange(G * tokens, dtype=jnp.int32) % tokens
    causal = jnp.arange(tokens, dtype=jnp.int32)[None, :] <= row_token[:, None]
    scores = jnp.where(causal[None], scores, -jnp.inf)
    top = jnp.max(scores, axis=-1)
    weights = jnp.exp(scores - top[..., None])
    total = jnp.sum(weights, axis=-1)
    summed = jnp.einsum(
        "krl,kld->krd", weights.astype(jnp.bfloat16), own_values, preferred_element_type=jnp.float32
    )
    carry = (top, total, summed)
    table_row = block_table[0]
    length = prefix_blocks[0]
    entries = table_row.shape[0]
    pool_count = lax.axis_size("blk")
    live_entry = jnp.arange(entries, dtype=jnp.int32) < length
    matches = (table_row[None, :] == jnp.arange(pool_count, dtype=jnp.int32)[:, None]) & live_entry[
        None, :
    ]
    used = jnp.any(matches, axis=1)
    state = carry
    piece_keys = lax.all_gather(prefix_keys, "blk", axis=0, tiled=True)
    piece_values = lax.all_gather(prefix_values, "blk", axis=0, tiled=True)
    count = piece_keys.shape[0] // BS
    key_blocks = piece_keys.reshape(count, BS, KVH, DH).transpose(0, 2, 1, 3)
    value_blocks = piece_values.reshape(count, BS, KVH, DH).transpose(0, 2, 1, 3)
    block_ids = jnp.arange(count, dtype=jnp.int32)

    def visit(inner, items):
        key_block, value_block, block_id = items
        return (absorb(inner, key_block, value_block, used[block_id], query_heads), None)

    state, _ = lax.scan(visit, state, (key_blocks, value_blocks, block_ids))
    carry = state
    top, total, summed = carry
    result = summed / total[..., None]
    result = result.reshape(KVH, G, tokens, DH).transpose(2, 0, 1, 3).reshape(tokens, KVH * G * DH)
    return result.astype(jnp.bfloat16)


def solution(mesh):
    in_specs = (
        P(("grp", "blk"), None),
        P(("grp", "blk"), None),
        P(("grp", "blk"), None),
        P(("grp", "blk"), None),
        P(("grp", "blk"), None),
        P(("grp", "blk"), None),
        P(("grp", "blk")),
    )
    out_specs = P(("grp", "blk"), None)
    return jax.shard_map(body, mesh=mesh, in_specs=in_specs, out_specs=out_specs, check_vma=False)
```

profile of v0, /device:TPU:1, one launch (start us, length us, event | category | flops | bytes accessed | tf_op | source)
XLA Modules:
  0.0 444.6 jit_solution(10240727030767275506)
XLA Ops:
  12.5 67.8 %all-gather.5.cloned.1.call-done = bf16[4096,512]{1,0:T(8,128)(2,1)} async-done(((bf16[128,512]{1,0:T(8,128)(2,1)}), bf16[4096,512]{1,0:T(8,128)(2,1)}) %all-gather.5.cloned.1.call-update) | async-done | bytes 4194320 | tf_op jit(solution)/shard_map/all_gather | solution.py:67
  80.3 6.9 %reshape.65 = bf16[32,128,4,128]{3,2,1,0:T(4,128)(2,1)} reshape(bf16[4096,512]{1,0:T(8,128)(2,1)} %all-gather.5.cloned.1.call-done) | data formatting | bytes 8388608 | tf_op jit(solution)/shard_map/reshape | solution.py:70
  87.2 5.3 %copy.57 = bf16[32,128,4,128]{3,1,2,0:T(8,128)(2,1)} copy(bf16[32,128,4,128]{3,2,1,0:T(4,128)(2,1)} %reshape.65) | data formatting | bytes 8388608 | tf_op jit(solution)/shard_map/transpose | solution.py:70
  92.5 56.1 %all-gather.3.cloned.1.call-done = bf16[4096,512]{1,0:T(8,128)(2,1)} async-done(((bf16[128,512]{1,0:T(8,128)(2,1)}), bf16[4096,512]{1,0:T(8,128)(2,1)}) %all-gather.3.cloned.1.call-update) | async-done | bytes 4194320 | tf_op jit(solution)/shard_map/all_gather | solution.py:66
  148.6 6.9 %reshape.64 = bf16[32,128,4,128]{3,2,1,0:T(4,128)(2,1)} reshape(bf16[4096,512]{1,0:T(8,128)(2,1)} %all-gather.3.cloned.1.call-done) | data formatting | bytes 8388608 | tf_op jit(solution)/shard_map/reshape | solution.py:69
  155.6 5.3 %copy.58 = bf16[32,128,4,128]{3,1,2,0:T(8,128)(2,1)} copy(bf16[32,128,4,128]{3,2,1,0:T(4,128)(2,1)} %reshape.64) | data formatting | bytes 8388608 | tf_op jit(solution)/shard_map/transpose | solution.py:69
  160.9 274.0 %while.14 = (s32[]{:T(128)}, f32[4,1024]{1,0:T(4,128)S(1)}, f32[4,1024]{1,0:T(4,128)S(1)}, f32[4,1024,128]{2,1,0:T(8,128)S(1)}, s32[32]{0:T(128)S(1)}, /*index=5...) while((s32[]{:T(128)}, f32[4,1024]{1,0:T(4,128)S(1)}, ...), condition=%wide.region_6.7_spmd, body=%wide.region_3.6_spmd.sunk | while | flops 275259392 | bytes 12060842 | solution.py:77
  166.7 2.7 multiply_add_fusion.5
  175.3 2.7 multiply_add_fusion.5
  183.9 2.7 multiply_add_fusion.5
  192.4 2.7 multiply_add_fusion.5
  209.6 2.7 multiply_add_fusion.5
  218.1 2.7 multiply_add_fusion.5
  226.7 2.7 multiply_add_fusion.5
  235.3 2.7 multiply_add_fusion.5
  243.8 2.7 multiply_add_fusion.5
  252.4 2.7 multiply_add_fusion.5
  260.9 2.7 multiply_add_fusion.5
  269.5 2.7 multiply_add_fusion.5
  278.1 2.7 multiply_add_fusion.5
  286.6 2.7 multiply_add_fusion.5
  295.2 2.7 multiply_add_fusion.5
  303.8 2.7 multiply_add_fusion.5
  312.3 2.7 multiply_add_fusion.5
  (262 shorter events, 179.7 us)
Async XLA Ops:
  6.5 4.2 copy-start
  6.5 73.8 %all-gather.5.cloned.1.call-start = ((), (), s32[]{:S(2)}) async-start(), calls=%async_computation.1 | async-start | bytes 4325376 | tf_op jit(solution)/shard_map/all_gather | solution.py:67
  7.3 141.4 %all-gather.3.cloned.1.call-start = ((), (), s32[]{:S(2)}) async-start(), calls=%async_computation | async-start | bytes 4325376 | tf_op jit(solution)/shard_map/all_gather | solution.py:66
  8.0 2.6 copy-start.2
  10.8 1.0 copy-start.1
Sparse Core Ops, SparseCore 0:
  9.2 71.0 all-gather.4
  82.2 66.4 all-gather.2
where the time goes:
time: 449 us; the launch traced here: 445 us
  matrix products  149 us (33%)
  waiting for transfers between devices  125 us (28%)
  local copies, waits for them, and re-layouts  64.4 us (14%)
  loops' own time  56.5 us (13%)
  other arithmetic  34.9 us (8%)
  between operations  14.2 us (3%)
    dot_general x32, matrix products, absorb(): jnp.einsum('krl,kld->krd', weights.astype(jnp.bfloat16), value_block, pre...  86.5 us
    all_gather x1, waiting for transfers between devices, body(): piece_values = lax.all_gather(prefix_values, 'blk', axis=0, tiled=True)  67.8 us
    dot_general x32, matrix products, absorb(): jnp.einsum('krd,kld->krl', query_heads, key_block, preferred_element_type...  61.6 us
    another operation x1, loops' own time, body(): state, _ = lax.scan(visit, state, (key_blocks, value_blocks, block_ids))  56.5 us
    all_gather x1, waiting for transfers between devices, body(): piece_keys = lax.all_gather(prefix_keys, 'blk', axis=0, tiled=True)  56.1 us
    reduce_sum x32, other arithmetic, absorb(): total = factor * total + jnp.sum(weights, axis=-1)  32.6 us
    dynamic_slice x32, local copies, waits for them, and re-layouts, visit(): used[block_id]  18 us
    dynamic_slice x32, local copies, waits for them, and re-layouts, body(): state, _ = lax.scan(visit, state, (key_blocks, value_blocks, block_ids))  17.9 us
  transfers between devices with their start and end apart: 2, of which 2 were waited for; matrix products, arithmetic and copies ran while one was open for 4% of the time, Pallas kernels for 0%

commit v1 on v0

--- a/solution.py
+++ b/solution.py
@@ -63,7 +63,10 @@
     ]
     used = jnp.any(matches, axis=1)
     state = carry
-    piece_keys = lax.all_gather(prefix_keys, "blk", axis=0, tiled=True)
+    tmp = lax.axis_size("blk")
+    kept_arr = jnp.stack(tmp * [prefix_keys])
+    reached = lax.all_to_all(kept_arr, axis_name="blk", split_axis=0, concat_axis=0)
+    piece_keys = jnp.concatenate(reached, axis=0)
     piece_values = lax.all_gather(prefix_values, "blk", axis=0, tiled=True)
     count = piece_keys.shape[0] // BS
     key_blocks = piece_keys.reshape(count, BS, KVH, DH).transpose(0, 2, 1, 3)

time: 449 us -> 427 us (0.951)
  waiting for transfers between devices: 125 us -> 97.7 us
  starting transfers between devices: 0.04 us -> 11.2 us
  local copies, waits for them, and re-layouts: 64.4 us -> 54.9 us
    all_gather x1 -> x0, waiting for transfers between devices: 56.1 us -> none  [body(): piece_keys = lax.all_gather(prefix_keys, 'blk', axis=0, tiled=True)]
    all_gather x1, waiting for transfers between devices: 67.8 us -> 93 us  [body(): piece_values = lax.all_gather(prefix_values, 'blk', axis=0, tiled=True)]
    all_to_all x0 -> x1, starting transfers between devices: none -> 11.2 us  [body(): lax.all_to_all(kept_arr, axis_name='blk', split_axis=0, concat_axis=0)]
    reshape x1 -> x0, local copies, waits for them, and re-layouts: 6.93 us -> none  [body(): key_blocks = piece_keys.reshape(count, BS, KVH, DH).transpose(0, 2, 1, 3)]
    transpose x1 -> x0, local copies, waits for them, and re-layouts: 5.33 us -> none  [body(): key_blocks = piece_keys.reshape(count, BS, KVH, DH).transpose(0, 2, 1, 3)]
where the time goes in v1:
time: 427 us; the launch traced here: 421 us
  matrix products  151 us (35%)
  waiting for transfers between devices  97.7 us (23%)
  loops' own time  56.5 us (13%)
  local copies, waits for them, and re-layouts  54.9 us (13%)
  other arithmetic  34.9 us (8%)
  between operations  14.2 us (3%)
  starting transfers between devices  11.2 us (3%)
    all_gather x1, waiting for transfers between devices, body(): piece_values = lax.all_gather(prefix_values, 'blk', axis=0, tiled=True)  93 us
    dot_general x32, matrix products, absorb(): jnp.einsum('krl,kld->krd', weights.astype(jnp.bfloat16), value_block, pre...  86.5 us
    dot_general x32, matrix products, absorb(): jnp.einsum('krd,kld->krl', query_heads, key_block, preferred_element_type...  63.4 us
    another operation x1, loops' own time, body(): state, _ = lax.scan(visit, state, (key_blocks, value_blocks, block_ids))  56.5 us
    reduce_sum x32, other arithmetic, absorb(): total = factor * total + jnp.sum(weights, axis=-1)  32.6 us
    dynamic_slice x32, local copies, waits for them, and re-layouts, visit(): used[block_id]  18 us
    dynamic_slice x32, local copies, waits for them, and re-layouts, body(): state, _ = lax.scan(visit, state, (key_blocks, value_blocks, block_ids))  17.9 us
    all_to_all x1, starting transfers between devices, body(): lax.all_to_all(kept_arr, axis_name='blk', split_axis=0, concat_axis=0)  11.2 us
  transfers between devices with their start and end apart: 2, of which 2 were waited for; matrix products, arithmetic and copies ran while one was open for 4% of the time, Pallas kernels for 0%

profile of v1, /device:TPU:1, one launch (start us, length us, event | category | flops | bytes accessed | tf_op | source)
XLA Modules:
  0.0 420.6 jit_solution(14548416305319080661)
XLA Ops:
  8.3 2.9 stack.2
  11.2 11.2 %all-to-all-start = ((bf16[32,128,512]{1,2,0:T(8,128)(2,1)}), bf16[32,128,512]{1,2,0:T(8,128)(2,1)}, u32[]{:S(2)}, u32[]{:S(2)}) async-start(bf16[32,128,512]{1,2,0:T(8,128)(2,1)} %stack.2), calls=%async_computation | async-start | bytes 8388608 | tf_op jit(solution)/shard_map/all_to_all | solution.py:68
  25.8 93.0 %all-gather.2.cloned.1.call-done = bf16[4096,512]{1,0:T(8,128)(2,1)} async-done(((bf16[128,512]{1,0:T(8,128)(2,1)}), bf16[4096,512]{1,0:T(8,128)(2,1)}) %all-gather.2.cloned.1.call-update) | async-done | bytes 4194320 | tf_op jit(solution)/shard_map/all_gather | solution.py:70
  118.8 6.9 %reshape.62 = bf16[32,128,4,128]{3,2,1,0:T(4,128)(2,1)} reshape(bf16[4096,512]{1,0:T(8,128)(2,1)} %all-gather.2.cloned.1.call-done) | data formatting | bytes 8388608 | tf_op jit(solution)/shard_map/reshape | solution.py:73
  125.7 5.3 %copy.55 = bf16[32,128,4,128]{3,1,2,0:T(8,128)(2,1)} copy(bf16[32,128,4,128]{3,2,1,0:T(4,128)(2,1)} %reshape.62) | data formatting | bytes 8388608 | tf_op jit(solution)/shard_map/transpose | solution.py:73
  131.1 4.0 all-to-all-done
  135.0 275.9 %while.14 = (s32[]{:T(128)}, f32[4,1024]{1,0:T(4,128)S(1)}, f32[4,1024]{1,0:T(4,128)S(1)}, f32[4,1024,128]{2,1,0:T(8,128)S(1)}, s32[32]{0:T(128)S(1)}, /*index=5...) while((s32[]{:T(128)}, f32[4,1024]{1,0:T(4,128)S(1)}, ...), condition=%wide.region_6.7_spmd, body=%wide.region_3.6_spmd.sunk | while | flops 275259392 | bytes 12060842 | solution.py:80
  158.2 2.7 multiply_add_fusion.5
  166.8 2.7 multiply_add_fusion.5
  175.4 2.7 multiply_add_fusion.5
  184.0 2.7 multiply_add_fusion.5
  192.7 2.7 multiply_add_fusion.5
  201.3 2.7 multiply_add_fusion.5
  209.9 2.7 multiply_add_fusion.5
  253.0 2.7 multiply_add_fusion.5
  261.6 2.7 multiply_add_fusion.5
  270.3 2.7 multiply_add_fusion.5
  278.9 2.7 multiply_add_fusion.5
  287.5 2.7 multiply_add_fusion.5
  330.6 2.7 multiply_add_fusion.5
  339.2 2.7 multiply_add_fusion.5
  347.9 2.7 multiply_add_fusion.5
  356.5 2.7 multiply_add_fusion.5
  365.1 2.7 multiply_add_fusion.5
  (263 shorter events, 180.6 us)
Async XLA Ops:
  6.5 17.5 %copy-start = (bf16[128,512]{1,0:T(8,128)(2,1)S(1)}, bf16[128,512]{1,0:T(8,128)(2,1)}, u32[]{:S(2)}) copy-start(bf16[128,512]{1,0:T(8,128)(2,1)} %param.10) | copy-start | bytes 393220
  6.5 112.3 %all-gather.2.cloned.1.call-start = ((), (), s32[]{:S(2)}) async-start(), calls=%async_computation.1 | async-start | bytes 4325376 | tf_op jit(solution)/shard_map/all_gather | solution.py:70
  11.2 11.2 %copy-start.1 = (bf16[128,4096]{1,0:T(8,128)(2,1)S(1)}, bf16[128,4096]{1,0:T(8,128)(2,1)}, u32[]{:S(2)}) copy-start(bf16[128,4096]{1,0:T(8,128)(2,1)} %param.9) | copy-start | bytes 3145732
  11.2 123.8 %all-to-all-start = ((bf16[32,128,512]{1,2,0:T(8,128)(2,1)}), bf16[32,128,512]{1,2,0:T(8,128)(2,1)}, u32[]{:S(2)}, u32[]{:S(2)}) async-start(bf16[32,128,512]{1,2,0:T(8,128)(2,1)} %stack.2), calls=%async_computation | async-start | bytes 8388608 | tf_op jit(solution)/shard_map/all_to_all | solution.py:68
  22.5 1.4 copy-start.3
  24.0 1.0 copy-start.2
Sparse Core Ops, SparseCore 0:
  9.2 109.5 all-gather.1
